TPU v7x, 512 devices: a whole 4x8x8 slice. The times are simulated.
512 devices in a mesh: seq: 64 (over x, y, z_lo), head: 8 (over z_hi, core).
Axes of the slice: x: 4, y: 8, z: 8 (z_hi: 4, z_lo: 2; z = z_hi * 2 + z_lo), core: 2. Of those that a mesh axis runs over, the one named last changes fastest.
Arguments:
- queries: bfloat16 [1, 65536, 2048], P(None, 'seq', 'head'), may hold values from -6 to 6
- keys: bfloat16 [1, 65536, 2048], P(None, 'seq', 'head'), may hold values from -6 to 6
- values: bfloat16 [1, 65536, 2048], P(None, 'seq', 'head'), may hold values from -6 to 6
- rates: float32 [1, 16, 65536], P(None, 'head', 'seq'), may hold values from 0.002 to 0.02
- decays: float32 [1, 16, 64], P(None, 'head'), may hold values from 0.02 to 1
- fast_in: bfloat16 [16, 128, 256], P('head'), may hold values from -5 to 5
- fast_out: bfloat16 [16, 128, 128], P('head'), may hold values from -0.5 to 0.5
- ttt_gain: float32 [2048], P('head'), may hold values from 0.25 to 1.75
- out_weight: bfloat16 [2048, 2048], P(None, 'head'), may hold values from -0.125 to 0.125
Outputs:
- layer_out: bfloat16 [1, 65536, 2048], P(None, 'seq', 'head')
All inputs are finite; a program needn't handle non-finite values.
Results may differ from a plain program's by a relative error of at most 0.017.
Values may be sent and summed in bfloat16 or wider, within the bound.
A program may use at most 128 MiB of HBM per device.

v0:
```python
import jax
import jax.numpy as jnp
from jax import lax
from jax.sharding import PartitionSpec as P

EPSILON = 1e-06


def passed_along(array, axis, by):
    peers = lax.axis_size(axis)
    pairs = [(i, i + by) for i in range(peers) if 0 <= i + by < peers]
    return lax.ppermute(array, axis, pairs)


def carried_in(part, axis, combine, identity):
    place = lax.axis_index(axis)
    gathered = jax.tree.map(lambda a: lax.all_gather(a, axis), part)
    state = jax.tree.map(lambda a, e: jnp.zeros_like(a) + jnp.asarray(e, a.dtype), part, identity)

    def one(lap, state):
        return combine(
            state, jax.tree.map(lambda a: lax.dynamic_index_in_dim(a, lap, 0, False), gathered)
        )

    return lax.fori_loop(0, place, one, state)


def unit_rows(matrix):
    widened = matrix.astype(jnp.float32)
    guarded = jnp.sum(widened * widened, axis=-1, keepdims=True) + EPSILON
    return (widened * lax.rsqrt(guarded)).astype(jnp.bfloat16)


def swish_product(raw_rows):
    half_width = raw_rows.shape[-1] // 2
    gate_part = raw_rows[..., :half_width]
    return gate_part * jax.nn.sigmoid(gate_part) * raw_rows[..., half_width:]


def local(queries, keys, values, rates, decays, fast_in, fast_out, ttt_gain, out_weight):
    seq_count, block_len, feat_width = queries.shape
    heads_here, head_size, double_hidden = fast_in.shape
    position = lax.axis_index("seq")
    received = []
    for offset in (1, 2):
        received.append(passed_along((keys, values), "seq", offset))
    near_tiles, far_tiles = received
    key_span = jnp.concatenate([far_tiles[0], near_tiles[0], keys], axis=1)
    value_span = jnp.concatenate([far_tiles[1], near_tiles[1], values], axis=1)
    divided_shape = (seq_count, block_len, heads_here, head_size)
    query_unit = unit_rows(queries.reshape(divided_shape))
    key_unit = unit_rows(keys.reshape(divided_shape))
    value_heads = values.reshape(divided_shape)
    raw_gate = jnp.einsum("schd,hdf->schf", key_unit, fast_in, preferred_element_type=jnp.float32)
    half_width = double_hidden // 2
    gate_part = raw_gate[..., :half_width]
    up_part = raw_gate[..., half_width:]
    gate_sigmoid = jax.nn.sigmoid(gate_part)
    hidden_keys = (gate_part * gate_sigmoid * up_part).astype(jnp.bfloat16)
    signal = (jnp.swapaxes(rates, 1, 2)[..., None] * value_heads.astype(jnp.float32)).astype(
        jnp.bfloat16
    )
    delta_out = jnp.einsum(
        "schf,schd->shfd", hidden_keys, signal, preferred_element_type=jnp.float32
    )
    back_signal = jnp.einsum("schd,hfd->schf", signal, fast_out, preferred_element_type=jnp.float32)
    grad_in = jnp.concatenate(
        [
            back_signal * up_part * gate_sigmoid * (1.0 + gate_part * (1.0 - gate_sigmoid)),
            back_signal * gate_part * gate_sigmoid,
        ],
        axis=-1,
    ).astype(jnp.bfloat16)
    delta_in = jnp.einsum("schd,schf->shdf", key_unit, grad_in, preferred_element_type=jnp.float32)
    own_decay = lax.dynamic_slice_in_dim(decays, position, 1, 2)[..., None]

    def compose(earlier, later):
        return (
            earlier[0] * later[0],
            later[0] * earlier[1] + later[1],
            later[0] * earlier[2] + later[2],
        )

    identity = (jnp.ones_like(own_decay), jnp.zeros_like(delta_in), jnp.zeros_like(delta_out))
    prefixed = carried_in((own_decay, delta_in, delta_out), "seq", compose, identity)
    carried, sum_in, sum_out = prefixed
    state_in = carried * fast_in.astype(jnp.float32)[None] + sum_in
    state_out = carried * fast_out.astype(jnp.float32)[None] + sum_out
    raw_query = jnp.einsum(
        "schd,shdf->schf",
        query_unit,
        state_in.astype(jnp.bfloat16),
        preferred_element_type=jnp.float32,
    )
    hidden_queries = swish_product(raw_query).astype(jnp.bfloat16)
    recalled = jnp.einsum(
        "schf,shfd->schd",
        hidden_queries,
        state_out.astype(jnp.bfloat16),
        preferred_element_type=jnp.float32,
    )
    mean_square = jnp.mean(recalled * recalled, axis=-1, keepdims=True) + EPSILON
    normed = recalled * lax.rsqrt(mean_square) * ttt_gain.reshape(heads_here, head_size)
    score_scale = head_size ** (-0.5)
    query_block = min(512, block_len)
    query_heads = queries.reshape(divided_shape)
    key_heads = key_span.reshape(seq_count, 3 * block_len, heads_here, head_size)
    value_span_heads = value_span.reshape(seq_count, 3 * block_len, heads_here, head_size)
    per_head = []
    for head_index in range(heads_here):
        segment_parts = []
        for row_start in range(0, block_len, query_block):
            query_part = query_heads[:, row_start : row_start + query_block, head_index]
            key_part = key_heads[:, row_start : row_start + 2 * block_len + query_block, head_index]
            value_part = value_span_heads[
                :, row_start : row_start + 2 * block_len + query_block, head_index
            ]
            scores = (
                jnp.einsum("sqd,skd->sqk", query_part, key_part, preferred_element_type=jnp.float32)
                * score_scale
            )
            query_pos = (
                position * block_len + row_start + lax.broadcasted_iota(jnp.int32, scores.shape, 1)
            )
            key_pos = (
                (position - 2) * block_len
                + row_start
                + lax.broadcasted_iota(jnp.int32, scores.shape, 2)
            )
            in_window = (
                (key_pos <= query_pos) & (key_pos > query_pos - 2 * block_len) & (key_pos >= 0)
            )
            masked = jnp.where(in_window, scores, -jnp.inf)
            highest = jnp.max(masked, axis=-1, keepdims=True)
            exp_scores = jnp.exp(masked - highest)
            weights = (exp_scores / jnp.sum(exp_scores, axis=-1, keepdims=True)).astype(
                jnp.bfloat16
            )
            segment_parts.append(
                jnp.einsum("sqk,skd->sqd", weights, value_part, preferred_element_type=jnp.float32)
            )
        per_head.append(jnp.concatenate(segment_parts, axis=1))
    attended = jnp.stack(per_head, axis=2)
    combined = (attended + normed).astype(jnp.bfloat16).reshape(seq_count, block_len, feat_width)
    portion = lax.all_gather(combined, "head", axis=2, tiled=True)
    projected = jnp.dot(
        portion.reshape(-1, portion.shape[2]), out_weight, preferred_element_type=jnp.float32
    )
    return projected.reshape(seq_count, block_len, -1).astype(jnp.bfloat16)


def solution(mesh):
    placed = (
        P(None, "seq", "head"),
        P(None, "seq", "head"),
        P(None, "seq", "head"),
        P(None, "head", "seq"),
        P(None, "head", None),
        P("head", None, None),
        P("head", None, None),
        P("head"),
        P(None, "head"),
    )
    return jax.shard_map(
        local, mesh=mesh, in_specs=placed, out_specs=P(None, "seq", "head"), check_vma=False
    )
```

profile of v0, /device:TPU:1, one launch (start us, length us, event | category | flops | bytes accessed | tf_op | source)
XLA Modules:
  0.0 1014.5 jit_solution(10808019783207171208)
XLA Ops:
  6.5 2.2 convert_multiply_fusion
  10.0 2.8 mul.215
  12.8 2.4 reduce_sum.67
  15.5 1.5 reshape.326
  17.4 1.3 copy-done.3
  18.8 2.5 fusion.31
  21.3 2.7 fusion.36
  26.4 4.9 collective-permute-start
  31.3 4.8 collective-permute-start.1
  36.3 2.3 collective-permute-start.2
  38.6 3.1 collective-permute-start.3
  43.1 1.6 reshape.327
  44.8 174.3 %all-gather = f32[64,2,1]{1,2,0:T(1,128)} all-gather(f32[1,2,1]{1,2,0:T(1,128)S(1)} %copy.196), channel_id=2, replica_groups=mesh['seq'=64,'head'=8] {'seq'}, dimensions={0}, use_global_device_ids=true | all-gather | bytes 520 | tf_op jit(solution)/shard_map/all_gather | solution.py:17
  219.3 1.5 pad_maximum_fusion
  220.8 1.8 fusion.53
  222.6 1.8 fusion.52
  229.3 1.8 fusion.51
  232.0 2.1 fusion.50
  236.8 85.4 %all-gather.11.cloned.1.call-done = f32[128,128,128]{2,1,0:T(8,128)} async-done(((f32[2,128,128]{2,1,0:T(8,128)}), f32[128,128,128]{2,1,0:T(8,128)}) %all-gather.11.cloned.1.call-update) | async-done | bytes 8388624 | tf_op jit(solution)/shard_map/all_gather | solution.py:17
  322.2 412.9 %all-gather.9.cloned.1.call-done = f32[128,128,256]{2,1,0:T(8,128)} async-done(((f32[2,128,256]{2,1,0:T(8,128)}), f32[128,128,256]{2,1,0:T(8,128)}) %all-gather.9.cloned.1.call-update) | async-done | bytes 16777232 | tf_op jit(solution)/shard_map/all_gather | solution.py:17
  735.3 1.7 convolution_bitcast_fusion
  737.0 1.6 multiply_reduce_fusion
  739.9 263.8 %all-gather.7.cloned.1.call-done = bf16[1,1024,2048]{1,2,0:T(8,128)(2,1)} async-done(((bf16[1,1024,256]{1,2,0:T(8,128)(2,1)}), bf16[1,1024,2048]{1,2,0:T(8,128)(2,1)}) %all-gather.7.cloned.1.call-update) | async-done | bytes 4194320 | tf_op jit(solution)/shard_map/all_gather | solution.py:145
  1003.7 4.3 fusion.14
  (63 shorter events, 15.9 us)
Async XLA Ops:
  6.5 997.2 %copy-start = (bf16[2048,256]{1,0:T(8,128)(2,1)S(1)}, bf16[2048,256]{1,0:T(8,128)(2,1)}, u32[]{:S(2)}) copy-start(bf16[2048,256]{1,0:T(8,128)(2,1)} %param.19) | copy-start | bytes 3145732
  6.5 8.9 copy-start.2
  6.5 10.4 %copy-start.4 = (bf16[2,128,256]{2,1,0:T(8,128)(2,1)S(1)}, bf16[2,128,256]{2,1,0:T(8,128)(2,1)}, u32[]{:S(2)}) copy-start(bf16[2,128,256]{2,1,0:T(8,128)(2,1)} %param.16) | copy-start | bytes 393220
  6.5 315.7 %all-gather.11.cloned.1.call-start = ((), (), s32[]{:S(2)}) async-start(), calls=%async_computation.2 | async-start | bytes 8519680 | tf_op jit(solution)/shard_map/all_gather | solution.py:17
  8.8 10.0 copy-start.8
  16.9 4.4 copy-start.7
  17.4 1.4 copy-start.3
  21.2 4.2 copy-start.1
  21.3 20.5 %copy-start.6 = (f32[1,2,64]{2,1,0:T(2,128)S(1)}, f32[1,2,64]{2,1,0:T(2,128)}, u32[]{:S(2)}) copy-start(f32[1,2,64]{2,1,0:T(2,128)} %param.15) | copy-start | bytes 1540
  21.3 713.9 %all-gather.9.cloned.1.call-start = ((), (), s32[]{:S(2)}) async-start(), calls=%async_computation.1 | async-start | bytes 17039360 | tf_op jit(solution)/shard_map/all_gather | solution.py:17
  25.4 978.4 %all-gather.7.cloned.1.call-start = ((), (), s32[]{:S(2)}) async-start(), calls=%async_computation | async-start | bytes 4718592 | tf_op jit(solution)/shard_map/all_gather | solution.py:145
  26.4 192.9 %collective-permute-start = (bf16[1,1024,256]{1,2,0:T(8,128)(2,1)}, bf16[1,1024,256]{1,2,0:T(8,128)(2,1)}, u32[]{:S(2)}, u32[]{:S(2)}) collective-permute-start(bf16[1,1024,256]{1,2,0:T(8,128)(2,1)} %copy.150), channel_id=1, source_target_pairs={{0,16},{8,24},{16,32},{24,40},{32,48},{40,56},{48,64},{56,72},{64,... | collective-permute-start | bytes 1572872 | tf_op jit(solution)/shard_map/ppermute | solution.py:12
  31.3 188.0 %collective-permute-start.1 = (bf16[1,1024,256]{1,2,0:T(8,128)(2,1)}, bf16[1,1024,256]{1,2,0:T(8,128)(2,1)}, u32[]{:S(2)}, u32[]{:S(2)}) collective-permute-start(bf16[1,1024,256]{1,2,0:T(8,128)(2,1)} %copy.150), channel_id=1, source_target_pairs={{0,8},{8,16},{16,24},{24,32},{32,40},{40,48},{48,56},{56,64},{64,7... | collective-permute-start | bytes 1572872 | tf_op jit(solution)/shard_map/ppermute | solution.py:12
  36.3 189.6 %collective-permute-start.2 = (bf16[1,1024,256]{1,2,0:T(8,128)(2,1)S(1)}, bf16[1,1024,256]{1,2,0:T(8,128)(2,1)}, u32[]{:S(2)}, u32[]{:S(2)}) collective-permute-start(bf16[1,1024,256]{1,2,0:T(8,128)(2,1)S(1)} %copy.156), channel_id=1, source_target_pairs={{0,16},{8,24},{16,32},{24,40},{32,48},{40,56},{48,64},{56,72},{64,... | collective-permute-start | bytes 1572872 | tf_op jit(solution)/shard_map/ppermute | solution.py:12
  38.6 187.3 %collective-permute-start.3 = (bf16[1,1024,256]{1,2,0:T(8,128)(2,1)S(1)}, bf16[1,1024,256]{1,2,0:T(8,128)(2,1)}, u32[]{:S(2)}, u32[]{:S(2)}) collective-permute-start(bf16[1,1024,256]{1,2,0:T(8,128)(2,1)S(1)} %copy.156), channel_id=1, source_target_pairs={{0,8},{8,16},{16,24},{24,32},{32,40},{40,48},{48,56},{56,64},{64,7... | collective-permute-start | bytes 1572872 | tf_op jit(solution)/shard_map/ppermute | solution.py:12
  735.2 3.3 copy-start.5
Sparse Core Ops, SparseCore 0:
  21.4 300.7 all-gather.10
  324.3 410.8 all-gather.8
  740.1 263.5 all-gather.6
where the time goes:
time: 1020 us; the launch traced here: 1010 us
  waiting for transfers between devices  762 us (75%)
  blocking collectives  174 us (17%)
  matrix products  26 us (3%)
  starting transfers between devices  15.2 us (1%)
  between operations  13.4 us (1%)
  local copies, waits for them, and re-layouts  12.3 us (1%)
  other arithmetic  11.1 us (1%)
    all_gather x2, waiting for transfers between devices, carried_in(): gathered = jax.tree.map(lambda a: lax.all_gather(a, axis), part)  498 us
    all_gather x1, waiting for transfers between devices, local(): portion = lax.all_gather(combined, 'head', axis=2, tiled=True)  264 us
    all_gather x1, blocking collectives, carried_in(): gathered = jax.tree.map(lambda a: lax.all_gather(a, axis), part)  174 us
  transfers between devices with their start and end apart: 7, of which 3 were waited for; matrix products, arithmetic and copies ran while one was open for 3% of the time, Pallas kernels for 0%

commit v1 on v0

v1 whole, which is shorter than its diff:
```python
import functools

import jax
import jax.numpy as jnp
from jax import lax
from jax.experimental import pallas as pl
from jax.experimental.pallas import tpu as pltpu
from jax.sharding import PartitionSpec as P

EPSILON = 1e-06
MESH = pl.DeviceIdType.MESH
F32 = jnp.float32
BF16 = jnp.bfloat16

PAIR = 2
COLUMN = 16
COLUMNS = 4
HEAD_DEVICES = 8
LOG2E = 1.4426950408889634

KV_CHUNKS = 8
GATHER_CHUNKS = 8
QUERY_ROWS = 256


def remote(src, dst, send_sem, recv_sem, device_id):
    return pltpu.make_async_remote_copy(
        src_ref=src,
        dst_ref=dst,
        send_sem=send_sem,
        recv_sem=recv_sem,
        device_id=device_id,
        device_id_type=MESH,
    )


def layer_kernel(
    q_ref, k_hbm, v_hbm, rates_ref, decays_ref, fin_ref, fout_ref, gain_ref, w_ref, o_ref,
    kv, rate_cols, dacc, dsend, drecv, tsend, trecv, ssend, states, gath,
    load_sem, far_send, far_recv, near_send, near_recv, d_send, d_recv,
    t_send, t_recv, s_send, s_recv, g_send, g_recv,
):
    place = lax.axis_index("seq")
    head_place = lax.axis_index("head")
    blocks = COLUMN * COLUMNS
    block_len = q_ref.shape[0]
    heads_here, dh = fin_ref.shape[0], fin_ref.shape[1]
    z_lo = lax.rem(place, PAIR)
    column = lax.div(place, COLUMN)
    rung = lax.rem(place, COLUMN)
    partner_block = place + 1 - 2 * z_lo
    two_on = lax.rem(place + 2, blocks)
    two_back = lax.rem(place + blocks - 2, blocks)
    z_hi = lax.div(head_place, 2)
    core = lax.rem(head_place, 2)
    right = lax.rem(z_hi + 1, 4) * 2 + core
    left = lax.rem(z_hi + 3, 4) * 2 + core
    across = lax.rem(z_hi + 2, 4) * 2 + core
    twin = z_hi * 2 + 1 - core

    def column_peer(step):
        return column * COLUMN + lax.rem(rung + step, COLUMN)

    def row_peer(step):
        return lax.rem(column + step, COLUMNS) * COLUMN + rung

    own_base = 2 * block_len
    loads = [
        pltpu.make_async_copy(k_hbm, kv.at[0, pl.ds(own_base, block_len)], load_sem.at[0]),
        pltpu.make_async_copy(v_hbm, kv.at[1, pl.ds(own_base, block_len)], load_sem.at[1]),
    ]
    for load in loads:
        load.start()
    barrier = pltpu.get_barrier_semaphore()
    for peer in (two_on, two_back):
        pl.semaphore_signal(barrier, inc=1, device_id={"seq": peer}, device_id_type=MESH)
    for peer in (left, right, twin):
        pl.semaphore_signal(barrier, inc=1, device_id={"head": peer}, device_id_type=MESH)

    def greet_column(step, _):
        pl.semaphore_signal(barrier, inc=1, device_id={"seq": column_peer(step)}, device_id_type=MESH)
        return 0

    def greet_row(step, _):
        pl.semaphore_signal(barrier, inc=1, device_id={"seq": row_peer(step)}, device_id_type=MESH)
        return 0

    lax.fori_loop(1, COLUMN, greet_column, 0)
    lax.fori_loop(1, COLUMNS, greet_row, 0)
    for load in loads:
        load.wait()
    pl.semaphore_wait(barrier, 2 + 3 + (COLUMN - 1) + (COLUMNS - 1))

    kv_rows = block_len // KV_CHUNKS

    def far_copy(c):
        rows = pl.multiple_of(c * kv_rows, kv_rows)
        return remote(
            kv.at[:, pl.ds(own_base + rows, kv_rows)],
            kv.at[:, pl.ds(rows, kv_rows)],
            far_send.at[c], far_recv.at[c], {"seq": two_on},
        )

    def near_copy(c, source_base):
        rows = pl.multiple_of(c * kv_rows, kv_rows)
        return remote(
            kv.at[:, pl.ds(source_base + rows, kv_rows)],
            kv.at[:, pl.ds(block_len + rows, kv_rows)],
            near_send.at[c], near_recv.at[c], {"seq": partner_block},
        )

    def send_kv(c, _):
        far_copy(c).start()

        @pl.when(z_lo == 0)
        def _():
            near_copy(c, own_base).start()

        return 0

    lax.fori_loop(0, KV_CHUNKS, send_kv, 0)

    def relay_kv(c, _):
        far_copy(c).wait_recv()

        @pl.when(z_lo == 1)
        def _():
            near_copy(c, 0).start()

        return 0

    rates8 = jnp.concatenate([rates_ref[...]] * 4, axis=0)
    rate_cols[...] = jnp.transpose(rates8)
    for h in range(heads_here):
        columns = slice(h * dh, (h + 1) * dh)
        w_in = fin_ref[h]
        w_out = fout_ref[h]
        for r in range(0, block_len, QUERY_ROWS):
            keys = kv[0, own_base + r : own_base + r + QUERY_ROWS, columns].astype(F32)
            values = kv[1, own_base + r : own_base + r + QUERY_ROWS, columns].astype(F32)
            norm = lax.rsqrt(jnp.sum(keys * keys, axis=-1, keepdims=True) + EPSILON)
            key_unit = (keys * norm).astype(BF16)
            raw = jnp.dot(key_unit, w_in, preferred_element_type=F32)
            gate, up = raw[:, :dh], raw[:, dh:]
            sig = jax.nn.sigmoid(gate)
            hidden = (gate * sig * up).astype(BF16)
            signal = (rate_cols[r : r + QUERY_ROWS, h : h + 1] * values).astype(BF16)
            back = lax.dot_general(signal, w_out, (((1,), (1,)), ((), ())), preferred_element_type=F32)
            grad = jnp.concatenate(
                [
                    (back * up * sig * (1.0 + gate * (1.0 - sig))).astype(BF16),
                    (back * gate * sig).astype(BF16),
                ],
                axis=-1,
            )
            d_in = lax.dot_general(key_unit, grad, (((0,), (0,)), ((), ())), preferred_element_type=F32)
            d_out = lax.dot_general(hidden, signal, (((0,), (0,)), ((), ())), preferred_element_type=F32)
            if r == 0:
                dacc[h, :, : 2 * dh] = d_in
                dacc[h, :, 2 * dh :] = d_out
            else:
                dacc[h, :, : 2 * dh] += d_in
                dacc[h, :, 2 * dh :] += d_out
    slices = dsend.shape[0]
    dsend[...] = dacc[...].reshape(dsend.shape).astype(BF16)

    def d_copy(step):
        target = lax.rem(rung + step, COLUMN)
        return remote(
            dsend.at[target], drecv.at[rung], d_send.at[step], d_recv.at[step],
            {"seq": column_peer(step)},
        )

    def d_wait(step, _):
        source = lax.rem(rung + COLUMN - step, COLUMN)
        remote(
            dsend.at[source], drecv.at[source], d_send.at[step], d_recv.at[step],
            {"seq": column_peer(step)},
        ).wait_recv()
        return 0

    def start(make):
        def one(step, _):
            make(step).start()
            return 0
        return one

    def drain(make):
        def one(step, _):
            make(step).wait_send()
            return 0
        return one

    lax.fori_loop(1, COLUMN, start(d_copy), 0)
    drecv[rung] = dsend[rung]

    lax.fori_loop(0, 4, relay_kv, 0)
    lax.fori_loop(1, COLUMN, d_wait, 0)

    slice_head = lax.div(rung, COLUMN // heads_here)

    def decay_at(index):
        return decays_ref[slice_head, index]

    def fold_in(i, total):
        return decay_at(column * COLUMN + i) * total + drecv[i].astype(F32)

    tsend[...] = lax.fori_loop(0, COLUMN, fold_in, jnp.zeros(tsend.shape, F32))

    def t_copy(step):
        return remote(
            tsend, trecv.at[column], t_send.at[step], t_recv.at[step], {"seq": row_peer(step)}
        )

    def t_wait(step, _):
        source = lax.rem(column + COLUMNS - step, COLUMNS)
        remote(
            tsend, trecv.at[source], t_send.at[step], t_recv.at[step], {"seq": row_peer(step)}
        ).wait_recv()
        return 0

    lax.fori_loop(1, COLUMNS, start(t_copy), 0)
    trecv[column] = tsend[...]
    lax.fori_loop(4, 6, relay_kv, 0)
    lax.fori_loop(1, COLUMNS, t_wait, 0)

    slice_row = lax.rem(rung, COLUMN // heads_here) * (dh * heads_here // COLUMN)
    slice_rows = pl.ds(pl.multiple_of(slice_row, 16), tsend.shape[0])
    state = jnp.concatenate(
        [fin_ref[slice_head, slice_rows].astype(F32), fout_ref[slice_head, slice_rows].astype(F32)], axis=-1
    )
    for c in range(COLUMNS - 1):
        kept = lax.fori_loop(0, COLUMN, lambda i, f: f * decay_at(c * COLUMN + i), jnp.float32(1.0))
        passed = c < column
        state = jnp.where(passed, kept, 1.0) * state + jnp.where(passed, 1.0, 0.0) * trecv[c]

    def advance(i, state):
        ssend[i] = state.astype(BF16)
        return decay_at(column * COLUMN + i) * state + drecv[i].astype(F32)

    lax.fori_loop(0, COLUMN, advance, state)

    def s_copy(step):
        target = lax.rem(rung + step, COLUMN)
        return remote(
            ssend.at[target], states.at[rung], s_send.at[step], s_recv.at[step],
            {"seq": column_peer(step)},
        )

    def s_wait(step, _):
        source = lax.rem(rung + COLUMN - step, COLUMN)
        remote(
            ssend.at[source], states.at[source], s_send.at[step], s_recv.at[step],
            {"seq": column_peer(step)},
        ).wait_recv()
        return 0

    lax.fori_loop(1, COLUMN, start(s_copy), 0)
    states[rung] = ssend[rung]
    lax.fori_loop(6, KV_CHUNKS, relay_kv, 0)

    def near_wait(c, _):
        near_copy(c, 0).wait_recv()
        return 0

    lax.fori_loop(1, COLUMN, s_wait, 0)
    lax.fori_loop(0, KV_CHUNKS, near_wait, 0)

    gather_rows = block_len // GATHER_CHUNKS
    pieces = QUERY_ROWS // gather_rows

    def gather_copy(kind, source, target, c):
        rows = pl.ds(pl.multiple_of(c * gather_rows, gather_rows), gather_rows)
        return remote(
            gath.at[source, rows], gath.at[source, rows],
            g_send.at[kind, c], g_recv.at[kind, c], {"head": target},
        )

    span = 2 * block_len + QUERY_ROWS
    first_valid = (2 - jnp.minimum(place, 2)) * block_len
    scale = LOG2E * dh ** (-0.5)

    def rows_of(rc, _):
        row0 = pl.multiple_of(rc * QUERY_ROWS, QUERY_ROWS)
        local_valid = first_valid - row0
        row_ids = lax.broadcasted_iota(jnp.int32, (QUERY_ROWS, QUERY_ROWS), 0)
        col_ids = lax.broadcasted_iota(jnp.int32, (QUERY_ROWS, QUERY_ROWS), 1)
        middle_ids = lax.broadcasted_iota(jnp.int32, (1, span - 2 * QUERY_ROWS), 1) + QUERY_ROWS
        middle_bias = jnp.where(middle_ids >= local_valid, 0.0, -1e30).astype(F32)
        for h in range(heads_here):
            columns = slice(h * dh, (h + 1) * dh)
            queries = q_ref[pl.ds(row0, QUERY_ROWS), columns]
            keys = kv[0, pl.ds(row0, span), columns]
            scores = lax.dot_general(queries, keys, (((1,), (1,)), ((), ())), preferred_element_type=F32)
            head_part = jnp.where(
                (col_ids > row_ids) & (col_ids >= local_valid), scores[:, :QUERY_ROWS], -1e30
            )
            middle_part = scores[:, QUERY_ROWS : span - QUERY_ROWS] + middle_bias
            tail_part = jnp.where(col_ids <= row_ids, scores[:, span - QUERY_ROWS :], -1e30)
            scores = jnp.concatenate([head_part, middle_part, tail_part], axis=-1)
            highest = jnp.max(scores, axis=-1, keepdims=True)
            weights = jnp.exp2((scores - highest) * scale).astype(BF16)
            values = kv[1, pl.ds(row0, span), columns]
            widened = jnp.concatenate([values, jnp.ones_like(values)], axis=-1)
            summed = jnp.dot(weights, widened, preferred_element_type=F32)
            attended = summed[:, :dh] / summed[:, dh:]

            q_wide = queries.astype(F32)
            q_norm = lax.rsqrt(jnp.sum(q_wide * q_wide, axis=-1, keepdims=True) + EPSILON)
            q_unit = (q_wide * q_norm).astype(BF16)
            per_head = COLUMN // heads_here
            state_h = states[h * per_head : (h + 1) * per_head].reshape(dh, 3 * dh)
            raw = jnp.dot(q_unit, state_h[:, : 2 * dh], preferred_element_type=F32)
            gate = raw[:, :dh]
            hidden = (gate * jax.nn.sigmoid(gate) * raw[:, dh:]).astype(BF16)
            recalled = jnp.dot(hidden, state_h[:, 2 * dh :], preferred_element_type=F32)
            mean_square = jnp.mean(recalled * recalled, axis=-1, keepdims=True) + EPSILON
            normed = recalled * lax.rsqrt(mean_square) * gain_ref[:, columns]
            gath[head_place, pl.ds(row0, QUERY_ROWS), columns] = (attended + normed).astype(BF16)
        for piece in range(pieces):
            c = rc * pieces + piece
            gather_copy(0, head_place, right, c).start()
            gather_copy(1, head_place, left, c).start()
            gather_copy(3, head_place, twin, c).start()
        return 0

    lax.fori_loop(0, block_len // QUERY_ROWS, rows_of, 0)

    left_twin = lax.rem(z_hi + 3, 4) * 2 + 1 - core
    right_twin = lax.rem(z_hi + 1, 4) * 2 + 1 - core
    across_twin = lax.rem(z_hi + 2, 4) * 2 + 1 - core

    def relay(c2, _):
        for odd in range(2):
            c = 2 * c2 + odd
            gather_copy(0, left, right, c).wait_recv()
            if odd == 0:
                gather_copy(2, left, right, c).start()
            gather_copy(4, left, twin, c).start()
            gather_copy(1, right, left, c).wait_recv()
            if odd == 1:
                gather_copy(2, right, left, c).start()
            gather_copy(5, right, twin, c).start()
        return 0

    lax.fori_loop(0, GATHER_CHUNKS // 2, relay, 0)

    def last_hop(c, _):
        gather_copy(2, across, left, c).wait_recv()
        gather_copy(6, across, twin, c).start()
        return 0

    lax.fori_loop(0, GATHER_CHUNKS, last_hop, 0)

    def project(c, _):
        gather_copy(3, twin, twin, c).wait_recv()
        gather_copy(4, left_twin, twin, c).wait_recv()
        gather_copy(5, right_twin, twin, c).wait_recv()
        gather_copy(6, across_twin, twin, c).wait_recv()
        rows = pl.ds(pl.multiple_of(c * gather_rows, gather_rows), gather_rows)
        width = gath.shape[2]
        total = jnp.zeros((gather_rows, width), F32)
        for h in range(HEAD_DEVICES):
            total += jnp.dot(
                gath[h, rows, :], w_ref[h * width : (h + 1) * width, :], preferred_element_type=F32
            )
        o_ref[rows, :] = total.astype(BF16)
        return 0

    lax.fori_loop(0, GATHER_CHUNKS, project, 0)

    def drain_kv(c, _):
        far_copy(c).wait_send()
        near_copy(c, 0).wait_send()
        return 0

    def drain_gather(c, _):
        for kind in range(7):
            gather_copy(kind, head_place, twin, c).wait_send()
        return 0

    lax.fori_loop(0, KV_CHUNKS, drain_kv, 0)
    lax.fori_loop(1, COLUMN, drain(d_copy), 0)
    lax.fori_loop(1, COLUMNS, drain(t_copy), 0)
    lax.fori_loop(1, COLUMN, drain(s_copy), 0)
    lax.fori_loop(0, GATHER_CHUNKS, drain_gather, 0)


def local(queries, keys, values, rates, decays, fast_in, fast_out, ttt_gain, out_weight):
    seq_count, block_len, width = queries.shape
    heads_here, dh, _ = fast_in.shape
    rows = heads_here * dh // COLUMN
    vmem = pl.BlockSpec(memory_space=pltpu.VMEM)
    smem = pl.BlockSpec(memory_space=pltpu.SMEM)
    anywhere = pl.BlockSpec(memory_space=pl.ANY)
    dma = pltpu.SemaphoreType.DMA
    out = pl.pallas_call(
        layer_kernel,
        out_shape=jax.ShapeDtypeStruct((block_len, width), BF16),
        in_specs=[vmem, anywhere, anywhere, vmem, smem, vmem, vmem, vmem, vmem],
        out_specs=vmem,
        scratch_shapes=[
            pltpu.VMEM((2, 3 * block_len, width), BF16),
            pltpu.VMEM((block_len, 8), F32),
            pltpu.VMEM((heads_here, dh, 3 * dh), F32),
            pltpu.VMEM((COLUMN, rows, 3 * dh), BF16),
            pltpu.VMEM((COLUMN, rows, 3 * dh), BF16),
            pltpu.VMEM((rows, 3 * dh), F32),
            pltpu.VMEM((COLUMNS, rows, 3 * dh), F32),
            pltpu.VMEM((COLUMN, rows, 3 * dh), BF16),
            pltpu.VMEM((COLUMN, rows, 3 * dh), BF16),
            pltpu.VMEM((HEAD_DEVICES, block_len, width), BF16),
            dma((2,)),
            dma((KV_CHUNKS,)), dma((KV_CHUNKS,)), dma((KV_CHUNKS,)), dma((KV_CHUNKS,)),
            dma((COLUMN,)), dma((COLUMN,)),
            dma((COLUMNS,)), dma((COLUMNS,)),
            dma((COLUMN,)), dma((COLUMN,)),
            dma((7, GATHER_CHUNKS)), dma((7, GATHER_CHUNKS)),
        ],
        compiler_params=pltpu.CompilerParams(
            collective_id=0, has_side_effects=True, vmem_limit_bytes=48 << 20
        ),
        name="layer",
    )(
        queries.reshape(block_len, width), keys.reshape(block_len, width), values.reshape(block_len, width),
        rates.reshape(heads_here, block_len), decays.reshape(heads_here, -1),
        fast_in, fast_out, ttt_gain.reshape(1, width), out_weight,
    )
    return out.reshape(seq_count, block_len, width)


def solution(mesh):
    placed = (
        P(None, "seq", "head"),
        P(None, "seq", "head"),
        P(None, "seq", "head"),
        P(None, "head", "seq"),
        P(None, "head", None),
        P("head", None, None),
        P("head", None, None),
        P("head"),
        P(None, "head"),
    )
    return jax.shard_map(
        local, mesh=mesh, in_specs=placed, out_specs=P(None, "seq", "head"), check_vma=False
    )
```

time: 1020 us -> 105 us (0.10)
  waiting for transfers between devices: 762 us -> 0 us
  blocking collectives: 174 us -> 0 us
  Pallas kernels: 0 us -> 97.3 us
  matrix products: 26 us -> 0 us
  starting transfers between devices: 15.2 us -> 0 us
  between operations: 13.4 us -> 0.02 us
  other arithmetic: 11.1 us -> 0 us
    all_gather x3 -> x0, waiting for transfers between devices: 762 us -> none  [the longest x2 498 us: carried_in(): gathered = jax.tree.map(lambda a: lax.all_gather(a, axis), part)]
    all_gather x1 -> x0, blocking collectives: 174 us -> none  [carried_in(): gathered = jax.tree.map(lambda a: lax.all_gather(a, axis), part)]
    pallas_call x0 -> x1, Pallas kernels: none -> 97.3 us  [local(): pl.pallas_call(layer_kernel, out_shape=jax.ShapeDtypeStruct((block_len, w...]
    dot_general x15 -> x0, matrix products: 26 us -> none  [the longest x4 7.6 us: local(): jnp.einsum('sqd,skd->sqk', query_part, key_part, preferred_element_type=j...]
    ppermute x4 -> x0, starting transfers between devices: 15.1 us -> none  [passed_along(): return lax.ppermute(array, axis, pairs)]
  transfers between devices with their start and end apart: 7 -> 0, of which waited for: 3 -> 0; matrix products, arithmetic and copies ran while one was open for 3% -> 0% of each run, Pallas kernels for 0% -> 0%
where the time goes in v1:
time: 105 us
  Pallas kernels  97.3 us (93%)
  local copies, waits for them, and re-layouts  7.59 us (7%)
    pallas_call x1, Pallas kernels, local(): pl.pallas_call(layer_kernel, out_shape=jax.ShapeDtypeStruct((block_len, w...  97.3 us
    unnamed x19, local copies, waits for them, and re-layouts  7.59 us

profile of v1, /device:TPU:1, one launch (start us, length us, event | category | flops | bytes accessed | tf_op | source)
XLA Modules:
  0.0 104.9 jit_solution(2229003254730032645)
XLA Ops:
  0.0 0.0 copy-start.6
  0.0 0.0 copy-start.8
  0.0 0.0 copy-start.7
  0.0 0.7 copy-done.6
  0.7 0.0 copy-done.8
  0.7 0.0 copy-done.7
  0.7 0.0 copy-start
  0.7 1.2 %copy-done = bf16[2048,256]{1,0:T(8,128)(2,1)S(1)} copy-done((bf16[2048,256]{1,0:T(8,128)(2,1)S(1)}, bf16[2048,256]{1,0:T(8,128)(2,1)}, u32[]{:S(2)}) %copy-start) | copy-done | bytes 1048600
  1.9 0.0 copy-start.1
  1.9 1.0 copy-done.1
  3.0 0.0 copy-start.2
  3.0 1.0 copy-done.2
  4.0 0.0 copy-start.3
  4.0 1.0 copy-done.3
  5.1 0.0 copy-start.4
  5.1 0.9 copy-done.4
  6.0 0.0 copy-start.5
  6.0 0.8 copy-done.5
  6.8 97.3 %layer.1 = bf16[1024,256]{1,0:T(8,128)(2,1)S(1)} custom-call(bf16[1024,256]{1,0:T(8,128)(2,1)S(1)} %bitcast.8, bf16[1024,256]{1,0:T(8,128)(2,1)S(1)} %bitcast.9, bf16[1024,256]{1,0:T(8,128)(2,1)S(1)} %bitcast.10, f32[2,1024]{1,0:T(2,128)S(1)} %bitcast.11, f32[2,64]{1,0:T(2,128)S(1)} %bitcast.12, bf16[2,128,256]{2,1,0:T(8,128)(2,1)S(1)} %copy-done.4, ...), custom_call_target="tpu_custom_call" | custom-call | tf_op jit(solution)/shard_map/layer/pallas_call | solution.py:397
  104.1 0.8 copy.11
Async XLA Ops:
  0.0 0.7 copy-start.6
  0.0 0.7 copy-start.8
  0.0 0.7 copy-start.7
  0.7 1.2 %copy-start = (bf16[2048,256]{1,0:T(8,128)(2,1)S(1)}, bf16[2048,256]{1,0:T(8,128)(2,1)}, u32[]{:S(2)}) copy-start(bf16[2048,256]{1,0:T(8,128)(2,1)} %w_ref.1) | copy-start | bytes 3145732
  1.9 1.0 copy-start.1
  3.0 1.0 copy-start.2
  4.0 1.0 copy-start.3
  5.1 0.9 copy-start.4
  6.0 0.8 copy-start.5

commit v2 on v0

v2 whole, which is shorter than its diff:
```python
import jax
import jax.numpy as jnp
from jax import lax
from jax.experimental import pallas as pl
from jax.experimental.pallas import tpu as pltpu
from jax.sharding import PartitionSpec as P

EPSILON = 1e-06
MESH = pl.DeviceIdType.MESH
F32 = jnp.float32
BF16 = jnp.bfloat16

COLUMN = 8
COLUMNS = 4
HEADS = 16
ROWS = 256
LOG2E = 1.4426950408889634


def remote(src, dst, send_sem, recv_sem, device_id):
    return pltpu.make_async_remote_copy(
        src_ref=src,
        dst_ref=dst,
        send_sem=send_sem,
        recv_sem=recv_sem,
        device_id=device_id,
        device_id_type=MESH,
    )


def dot(a, b):
    return jnp.dot(a, b, preferred_element_type=F32)


def dot_nt(a, b):
    return lax.dot_general(a, b, (((1,), (1,)), ((), ())), preferred_element_type=F32)


def dot_tn(a, b):
    return lax.dot_general(a, b, (((0,), (0,)), ((), ())), preferred_element_type=F32)


def layer_kernel(
    q_hbm, k_hbm, v_hbm, rates_hbm, decays_ref, fin_hbm, fout_hbm, gain_hbm, w_hbm, o_ref,
    kv, qh, spare, rates_ref, rate_cols, fin_ref, fout_ref, gain_ref, w_ref,
    dsend, dpair, tsend, trecv, usend, urecv, ssend, srecv, states, comb, gath,
    load_sem, pair_sem, q_send, q_recv, e_send, e_recv, far_send, far_recv, t_send, t_recv,
    u_send, u_recv, s_send, s_recv, g_send, g_recv,
):
    place = lax.axis_index("seq")
    head_place = lax.axis_index("head")
    blocks = 2 * COLUMN * COLUMNS
    block_len = q_hbm.shape[0]
    dh = fin_ref.shape[1]
    pieces = block_len // ROWS
    z_lo = lax.rem(place, 2)
    pair = lax.div(place, 2)
    rung = lax.rem(pair, COLUMN)
    column = lax.div(pair, COLUMN)
    z_hi = lax.div(head_place, 2)
    core = lax.rem(head_place, 2)
    partner = place + 1 - 2 * z_lo
    two_on = lax.rem(place + 2, blocks)
    two_back = lax.rem(place + blocks - 2, blocks)

    def at(hops, which):
        return lax.rem(z_hi + hops + 8, 4) * 2 + which

    def head_of(hops, which, low):
        return lax.rem(z_hi + hops + 8, 4) * 4 + which * 2 + low

    up2 = {"head": at(1, core)}
    down2 = {"head": at(-1, core)}
    twin = {"head": at(0, 1 - core)}
    up1 = {"seq": partner, "head": at(z_lo, core)}
    down1 = {"seq": partner, "head": at(z_lo - 1, core)}

    def column_peer(step):
        return {"seq": (column * COLUMN + lax.rem(rung + step, COLUMN)) * 2 + z_lo}

    def row_peer(step):
        return {"seq": (lax.rem(column + step, COLUMNS) * COLUMN + rung) * 2 + z_lo}

    mine = pl.ds(pl.multiple_of(z_lo * dh, dh), dh)
    other = pl.ds(pl.multiple_of((1 - z_lo) * dh, dh), dh)
    own_row = pl.multiple_of(z_lo * block_len, block_len)
    own_base = pl.multiple_of(2 * block_len + z_lo * block_len, block_len)
    own_rows = pl.ds(own_base, block_len)
    load_list = [
        (k_hbm.at[:, mine], kv.at[0, own_rows]),
        (v_hbm.at[:, mine], kv.at[1, own_rows]),
        (k_hbm.at[:, other], spare.at[0]),
        (v_hbm.at[:, other], spare.at[1]),
        (rates_hbm, rates_ref),
        (fin_hbm, fin_ref),
        (fout_hbm, fout_ref),
        (q_hbm.at[:, other], spare.at[2]),
        (q_hbm.at[:, mine], qh.at[pl.ds(own_row, block_len)]),
        (gain_hbm, gain_ref),
        (w_hbm, w_ref),
    ]
    loads = [
        pltpu.make_async_copy(src, dst, load_sem.at[i]) for i, (src, dst) in enumerate(load_list)
    ]
    for load in loads:
        load.start()

    barrier = pltpu.get_barrier_semaphore()

    def greet(device_id):
        pl.semaphore_signal(barrier, inc=1, device_id=device_id, device_id_type=MESH)

    def greet_column(step, _):
        greet(column_peer(step))
        return 0

    def greet_row(step, _):
        greet(row_peer(step))
        return 0

    lax.fori_loop(1, COLUMN, greet_column, 0)
    lax.fori_loop(1, COLUMNS, greet_row, 0)
    for device_id in ({"seq": two_on}, {"seq": two_back}, up1, down1, up2, down2, twin):
        greet(device_id)
    for load in loads[:7]:
        load.wait()

    lower = z_lo == 0
    rates_mine = jnp.where(lower, rates_ref[0:1, :], rates_ref[1:2, :])
    rates_other = jnp.where(lower, rates_ref[1:2, :], rates_ref[0:1, :])
    rate_cols[...] = jnp.transpose(jnp.concatenate([rates_mine, rates_other] * 4, axis=0))
    for which in (1, 0):
        w_in = fin_ref[1 - z_lo] if which else fin_ref[z_lo]
        w_out = fout_ref[1 - z_lo] if which else fout_ref[z_lo]
        d_in = d_out = None
        for r in range(0, block_len, ROWS):
            if which:
                keys, values = spare[0, r : r + ROWS], spare[1, r : r + ROWS]
            else:
                rows = pl.ds(pl.multiple_of(own_base + r, ROWS), ROWS)
                keys, values = kv[0, rows], kv[1, rows]
            keys, values = keys.astype(F32), values.astype(F32)
            norm = lax.rsqrt(jnp.sum(keys * keys, axis=-1, keepdims=True) + EPSILON)
            key_unit = (keys * norm).astype(BF16)
            raw = dot(key_unit, w_in)
            gate, up = raw[:, :dh], raw[:, dh:]
            sig = jax.nn.sigmoid(gate)
            hidden = (gate * sig * up).astype(BF16)
            signal = (rate_cols[r : r + ROWS, which : which + 1] * values).astype(BF16)
            back = dot_nt(signal, w_out)
            grad = jnp.concatenate(
                [
                    (back * up * sig * (1.0 + gate * (1.0 - sig))).astype(BF16),
                    (back * gate * sig).astype(BF16),
                ],
                axis=-1,
            )
            part_in, part_out = dot_tn(key_unit, grad), dot_tn(hidden, signal)
            d_in = part_in if d_in is None else d_in + part_in
            d_out = part_out if d_out is None else d_out + part_out
        delta = jnp.concatenate([d_in, d_out], axis=-1).astype(BF16)
        if which:
            dsend[...] = delta
        else:
            dpair[z_lo] = delta

    pl.semaphore_wait(barrier, (COLUMN - 1) + (COLUMNS - 1) + 7)

    pair_device = {"seq": partner}

    def start(make):
        def one(step, _):
            make(step).start()
            return 0
        return one

    def wait_sent(make):
        def one(step, _):
            make(step).wait_send()
            return 0
        return one

    def wait_got(make):
        def one(step, _):
            make(step).wait_recv()
            return 0
        return one

    d_copy = remote(dsend, dpair.at[z_lo], pair_sem.at[0], pair_sem.at[1], pair_device)

    def q_copy(i):
        row = pl.multiple_of(i * ROWS, ROWS)
        return remote(
            spare.at[2, pl.ds(row, ROWS)],
            qh.at[pl.ds(pl.multiple_of(own_row + row, ROWS), ROWS)],
            q_send.at[i], q_recv.at[i], pair_device,
        )

    def e_copy(i):
        row = pl.multiple_of(i * ROWS, ROWS)
        return remote(
            spare.at[pl.ds(0, 2), pl.ds(row, ROWS)],
            kv.at[:, pl.ds(pl.multiple_of(own_base + row, ROWS), ROWS)],
            e_send.at[i], e_recv.at[i], pair_device,
        )

    def far_copy(c):
        row = pl.multiple_of(c * ROWS, ROWS)
        return remote(
            kv.at[:, pl.ds(pl.multiple_of(2 * block_len + row, ROWS), ROWS)],
            kv.at[:, pl.ds(row, ROWS)],
            far_send.at[c], far_recv.at[c], {"seq": two_on},
        )

    def relay_far(i):
        e_copy(i).wait_recv()
        far_copy((1 - z_lo) * pieces + i).start()

    d_copy.start()

    far_copy((1 + z_lo) * pieces - 1).start()

    loads[7].wait()
    for i in reversed(range(pieces)):
        e_copy(i).start()
    for i in reversed(range(pieces)):
        q_copy(i).start()

    def decay_at(block):
        return decays_ref[z_lo, block]

    def pair_decay(c, r):
        first = (c * COLUMN + r) * 2
        return decay_at(first) * decay_at(first + 1)

    d_copy.wait_recv()
    pair_sum = decay_at(2 * pair + 1) * dpair[0].astype(F32) + dpair[1].astype(F32)
    tsend[...] = pair_sum.astype(BF16).reshape(tsend.shape)

    def t_copy(step):
        target = lax.rem(rung + step, COLUMN)
        return remote(
            tsend.at[target], trecv.at[rung], t_send.at[step], t_recv.at[step], column_peer(step)
        )

    lax.fori_loop(1, COLUMN, start(t_copy), 0)
    trecv[rung] = tsend[rung]

    @pl.when(z_lo == 1)
    def _():
        far_copy(2 * pieces - 2).start()
        far_copy(2 * pieces - 3).start()

    @pl.when(z_lo == 0)
    def _():
        relay_far(3)

    lax.fori_loop(1, COLUMN, wait_got(t_copy), 0)

    def fold_in(r, total):
        return pair_decay(column, r) * total + trecv[r].astype(F32)

    usend[...] = lax.fori_loop(0, COLUMN, fold_in, jnp.zeros(usend.shape, F32))

    def u_copy(step):
        return remote(usend, urecv.at[column], u_send.at[step], u_recv.at[step], row_peer(step))

    lax.fori_loop(1, COLUMNS, start(u_copy), 0)
    urecv[column] = usend[...]

    @pl.when(z_lo == 0)
    def _():
        relay_far(2)

    slice_rows = pl.ds(pl.multiple_of(rung * (dh // COLUMN), dh // COLUMN), dh // COLUMN)
    state = jnp.concatenate(
        [fin_ref[z_lo, slice_rows].astype(F32), fout_ref[z_lo, slice_rows].astype(F32)], axis=-1
    )
    kept = [
        lax.fori_loop(0, COLUMN, lambda r, f: f * pair_decay(c, r), jnp.float32(1.0))
        for c in range(COLUMNS - 1)
    ]
    lax.fori_loop(1, COLUMNS, wait_got(u_copy), 0)
    for c in range(COLUMNS - 1):
        passed = c < column
        state = jnp.where(passed, kept[c], 1.0) * state + jnp.where(passed, 1.0, 0.0) * urecv[c]

    def advance(r, state):
        ssend[r] = state.astype(BF16)
        return pair_decay(column, r) * state + trecv[r].astype(F32)

    lax.fori_loop(0, COLUMN, advance, state)

    def s_copy(step):
        target = lax.rem(rung + step, COLUMN)
        return remote(
            ssend.at[target], srecv.at[rung], s_send.at[step], s_recv.at[step], column_peer(step)
        )

    lax.fori_loop(1, COLUMN, start(s_copy), 0)
    srecv[rung] = ssend[rung]

    @pl.when(z_lo == 1)
    def _():
        far_copy(2 * pieces - 4).start()
        relay_far(3)
        relay_far(2)

    relay_far(1)
    relay_far(0)

    @pl.when(z_lo == 0)
    def _():
        for i in reversed(range(pieces - 1)):
            far_copy(i).start()

    span = 2 * block_len + ROWS
    first_valid = jnp.where(pair == 0, 2 * block_len, 0)
    scale = LOG2E * dh ** (-0.5)

    def attend(j):
        row0 = pl.multiple_of(j * ROWS, ROWS)
        local_valid = first_valid - row0
        row_ids = lax.broadcasted_iota(jnp.int32, (ROWS, ROWS), 0)
        col_ids = lax.broadcasted_iota(jnp.int32, (ROWS, ROWS), 1)
        middle_ids = lax.broadcasted_iota(jnp.int32, (1, span - 2 * ROWS), 1) + ROWS
        middle_bias = jnp.where(middle_ids >= local_valid, 0.0, -1e30).astype(F32)
        scores = dot_nt(qh[pl.ds(row0, ROWS)], kv[0, pl.ds(row0, span)])
        head_part = jnp.where(
            (col_ids > row_ids) & (col_ids >= local_valid), scores[:, :ROWS], -1e30
        )
        middle_part = scores[:, ROWS : span - ROWS] + middle_bias
        tail_part = jnp.where(col_ids <= row_ids, scores[:, span - ROWS :], -1e30)
        scores = jnp.concatenate([head_part, middle_part, tail_part], axis=-1)
        highest = jnp.max(scores, axis=-1, keepdims=True)
        weights = jnp.exp2((scores - highest) * scale).astype(BF16)
        values = kv[1, pl.ds(row0, span)]
        summed = dot(weights, jnp.concatenate([values, jnp.ones_like(values)], axis=-1))
        return summed[:, :dh] / summed[:, dh:]

    def recall(j, parity):
        queries = qh[pl.ds(pl.multiple_of(j * ROWS, ROWS), ROWS)].astype(F32)
        norm = lax.rsqrt(jnp.sum(queries * queries, axis=-1, keepdims=True) + EPSILON)
        raw = dot((queries * norm).astype(BF16), states[parity, :, : 2 * dh])
        gate = raw[:, :dh]
        hidden = (gate * jax.nn.sigmoid(gate) * raw[:, dh:]).astype(BF16)
        recalled = dot(hidden, states[parity, :, 2 * dh :])
        mean_square = jnp.mean(recalled * recalled, axis=-1, keepdims=True) + EPSILON
        return recalled * lax.rsqrt(mean_square) * gain

    def arrivals(which):
        return (
            head_of(-1, which, z_lo), head_of(1, which, z_lo), head_of(2, which, z_lo),
            head_of(z_lo - 1, which, 1 - z_lo), head_of(z_lo, which, 1 - z_lo),
            head_of(z_lo - 2, which, 1 - z_lo), head_of(z_lo + 1, which, 1 - z_lo),
        )

    own_head = head_of(0, core, z_lo)
    twin_head = head_of(0, 1 - core, z_lo)
    heads_in = arrivals(core)
    twin_heads = (twin_head,) + arrivals(1 - core)

    def piece_of(i):
        return pl.ds(pl.multiple_of(i * ROWS, ROWS), ROWS)

    def g_copy(kind, src, head, i, device_id):
        return remote(src, gath.at[head, piece_of(i)], g_send.at[kind, i], g_recv.at[kind, i], device_id)

    def pass_on(kind, from_kind, i, device_id):
        head = heads_in[from_kind]
        return g_copy(kind, gath.at[head, piece_of(i)], head, i, device_id)

    def got(kind, i):
        head = heads_in[kind] if kind < 7 else twin_heads[kind - 7]
        g_copy(kind, gath.at[head, piece_of(i)], head, i, twin).wait_recv()

    def finish(j, attended, parity):
        i = j - parity * pieces
        row = piece_of(i)
        mixed = (attended + recall(j, parity)).astype(BF16)
        comb[parity, row] = mixed
        src = comb.at[parity, row]

        @pl.when(z_lo == parity)
        def _():
            gath[own_head, row] = mixed
            g_copy(0, src, own_head, i, up2).start()
            g_copy(1, src, own_head, i, down2).start()
            g_copy(7, src, own_head, i, twin).start()

        @pl.when(z_lo != parity)
        def _():
            g_copy(3, src, own_head, i, up1).start()
            g_copy(4, src, own_head, i, down1).start()

    loads[8].wait()
    loads[9].wait()
    gain = jnp.where(lower, gain_ref[:, :dh], gain_ref[:, dh:])
    lax.fori_loop(1, COLUMN, wait_got(s_copy), 0)
    states[0] = srecv[...].reshape(dh, 3 * dh)
    states[1] = (decay_at(2 * pair) * states[0].astype(F32) + dpair[0].astype(F32)).astype(BF16)

    for parity in (1, 0):

        def one(step, _):
            i = pieces - 1 - step
            j = i + parity * pieces

            @pl.when(z_lo != parity)
            def _():
                q_copy(i).wait_recv()

            far_copy(j).wait_recv()
            finish(j, attend(j), parity)
            return 0

        lax.fori_loop(0, pieces, one, 0)

    def relay(step, _):
        for odd in (1, 0):
            i = pieces - 2 - 2 * step + odd
            got(0, i)
            if odd == 0:
                pass_on(2, 0, i, up2).start()
            pass_on(8, 0, i, twin).start()
            got(1, i)
            if odd == 1:
                pass_on(2, 1, i, down2).start()
            pass_on(9, 1, i, twin).start()
            got(3, i)
            pass_on(5, 3, i, up2).start()
            pass_on(11, 3, i, twin).start()
            got(4, i)
            pass_on(6, 4, i, down2).start()
            pass_on(12, 4, i, twin).start()
        return 0

    lax.fori_loop(0, pieces // 2, relay, 0)

    def last_hop(step, _):
        i = pieces - 1 - step
        for kind in (2, 5, 6):
            got(kind, i)
            pass_on(kind + 8, kind, i, twin).start()
        return 0

    lax.fori_loop(0, pieces, last_hop, 0)
    loads[10].wait()

    def project(step, _):
        i = pieces - 1 - step
        for kind in range(7, 15):
            got(kind, i)
        row = piece_of(i)
        total = jnp.zeros((ROWS, o_ref.shape[1]), F32)
        for g in range(0, HEADS, 2):
            both = jnp.concatenate([gath[g, row], gath[g + 1, row]], axis=-1)
            total += dot(both, w_ref[g * dh : (g + 2) * dh, :])
        o_ref[row, :] = total.astype(BF16)
        return 0

    lax.fori_loop(0, pieces, project, 0)

    d_copy.wait_send()

    def drain_gather(i, _):
        for kind in range(15):
            g_copy(kind, comb.at[0, piece_of(i)], own_head, i, twin).wait_send()
        return 0

    lax.fori_loop(0, pieces, wait_sent(e_copy), 0)
    lax.fori_loop(0, pieces, wait_sent(q_copy), 0)
    lax.fori_loop(0, 2 * pieces, wait_sent(far_copy), 0)
    lax.fori_loop(1, COLUMN, wait_sent(t_copy), 0)
    lax.fori_loop(1, COLUMNS, wait_sent(u_copy), 0)
    lax.fori_loop(1, COLUMN, wait_sent(s_copy), 0)
    lax.fori_loop(0, pieces, drain_gather, 0)


def local(queries, keys, values, rates, decays, fast_in, fast_out, ttt_gain, out_weight):
    seq_count, block_len, width = queries.shape
    heads_here, dh, _ = fast_in.shape
    pieces = block_len // ROWS
    state_shape = (dh, 3 * dh)
    slices_shape = (COLUMN, dh // COLUMN, 3 * dh)
    hbm = pl.BlockSpec(memory_space=pltpu.HBM)
    dma = pltpu.SemaphoreType.DMA
    vmem = pltpu.VMEM
    out = pl.pallas_call(
        layer_kernel,
        out_shape=jax.ShapeDtypeStruct((block_len, width), BF16),
        in_specs=[hbm, hbm, hbm, hbm, pl.BlockSpec(memory_space=pltpu.SMEM), hbm, hbm, hbm, hbm],
        out_specs=pl.BlockSpec(memory_space=pltpu.VMEM),
        scratch_shapes=[
            vmem((2, 4 * block_len, dh), BF16),
            vmem((2 * block_len, dh), BF16),
            vmem((3, block_len, dh), BF16),
            vmem((heads_here, block_len), F32),
            vmem((block_len, 8), F32),
            vmem(fast_in.shape, BF16),
            vmem(fast_out.shape, BF16),
            vmem((1, width), F32),
            vmem(out_weight.shape, BF16),
            vmem(state_shape, BF16),
            vmem((2,) + state_shape, BF16),
            vmem(slices_shape, BF16),
            vmem(slices_shape, BF16),
            vmem(slices_shape[1:], F32),
            vmem((COLUMNS,) + slices_shape[1:], F32),
            vmem(slices_shape, BF16),
            vmem(slices_shape, BF16),
            vmem((2,) + state_shape, BF16),
            vmem((2, block_len, dh), BF16),
            vmem((HEADS, block_len, dh), BF16),
            dma((11,)), dma((2,)),
            dma((pieces,)), dma((pieces,)),
            dma((pieces,)), dma((pieces,)), dma((2 * pieces,)), dma((2 * pieces,)),
            dma((COLUMN,)), dma((COLUMN,)), dma((COLUMNS,)), dma((COLUMNS,)),
            dma((COLUMN,)), dma((COLUMN,)),
            dma((15, pieces)), dma((15, pieces)),
        ],
        compiler_params=pltpu.CompilerParams(
            collective_id=0, has_side_effects=True, vmem_limit_bytes=63 << 20
        ),
        name="layer",
    )(
        queries.reshape(block_len, width), keys.reshape(block_len, width), values.reshape(block_len, width),
        rates.reshape(heads_here, block_len), decays.reshape(heads_here, -1),
        fast_in, fast_out, ttt_gain.reshape(1, width), out_weight,
    )
    return out.reshape(seq_count, block_len, width)


def solution(mesh):
    placed = (
        P(None, "seq", "head"),
        P(None, "seq", "head"),
        P(None, "seq", "head"),
        P(None, "head", "seq"),
        P(None, "head", None),
        P("head", None, None),
        P("head", None, None),
        P("head"),
        P(None, "head"),
    )
    return jax.shard_map(
        local, mesh=mesh, in_specs=placed, out_specs=P(None, "seq", "head"), check_vma=False
    )
```

time: 1020 us -> 80.8 us (0.08)
  waiting for transfers between devices: 762 us -> 0 us
  blocking collectives: 174 us -> 0 us
  Pallas kernels: 0 us -> 78.7 us
  matrix products: 26 us -> 0 us
  starting transfers between devices: 15.2 us -> 0 us
  between operations: 13.4 us -> 0.01 us
  other arithmetic: 11.1 us -> 0 us
  local copies, waits for them, and re-layouts: 12.3 us -> 1.87 us
    all_gather x3 -> x0, waiting for transfers between devices: 762 us -> none  [the longest x2 498 us: carried_in(): gathered = jax.tree.map(lambda a: lax.all_gather(a, axis), part)]
    all_gather x1 -> x0, blocking collectives: 174 us -> none  [carried_in(): gathered = jax.tree.map(lambda a: lax.all_gather(a, axis), part)]
    pallas_call x0 -> x1, Pallas kernels: none -> 78.7 us  [local(): pl.pallas_call(layer_kernel, out_shape=jax.ShapeDtypeStruct((block_len, w...]
    dot_general x15 -> x0, matrix products: 26 us -> none  [the longest x4 7.6 us: local(): jnp.einsum('sqd,skd->sqk', query_part, key_part, preferred_element_type=j...]
    ppermute x4 -> x0, starting transfers between devices: 15.1 us -> none  [passed_along(): return lax.ppermute(array, axis, pairs)]
  transfers between devices with their start and end apart: 7 -> 0, of which waited for: 3 -> 0; matrix products, arithmetic and copies ran while one was open for 3% -> 0% of each run, Pallas kernels for 0% -> 0%
where the time goes in v2:
time: 80.8 us; the launch traced here: 80.6 us
  Pallas kernels  78.7 us (97%)
  local copies, waits for them, and re-layouts  1.87 us (2%)
    pallas_call x1, Pallas kernels, local(): pl.pallas_call(layer_kernel, out_shape=jax.ShapeDtypeStruct((block_len, w...  78.7 us
    unnamed x1, local copies, waits for them, and re-layouts  1.87 us

profile of v2, /device:TPU:1, one launch (start us, length us, event | category | flops | bytes accessed | tf_op | source)
XLA Modules:
  0.0 80.6 jit_solution(5110949636689659803)
XLA Ops:
  0.0 78.7 %layer.1 = bf16[1024,256]{1,0:T(8,128)(2,1)} custom-call(bf16[1024,256]{1,0:T(8,128)(2,1)} %bitcast.8, bf16[1024,256]{1,0:T(8,128)(2,1)} %bitcast.9, bf16[1024,256]{1,0:T(8,128)(2,1)} %bitcast.10, f32[2,1024]{1,0:T(2,128)} %bitcast.11, f32[2,64]{1,0:T(2,128)} %bitcast.12, bf16[2,128,256]{2,1,0:T(8,128)(2,1)} %fin_hbm.1, bf16[2,128,128]{2,1,0:T(8,128)(2,1)} %fout_hbm.1, ...), custom_call_target="tpu_custom_call" | custom-call | tf_op jit(solution)/shard_map/layer/pallas_call | solution.py:489
  78.7 1.9 %copy.11 = bf16[1,1024,256]{2,1,0:T(8,128)(2,1)} copy(bf16[1,1024,256]{2,1,0:T(8,128)(2,1)} %bitcast.7) | data formatting | bytes 1048576

commit v3 on v2

--- a/solution.py
+++ b/solution.py
@@ -15,6 +15,11 @@
 HEADS = 16
 ROWS = 256
 LOG2E = 1.4426950408889634
+
+EARLY = {4: 3, 0: 2}
+
+UPPER_STOPS = (0, 1, 3, 3, 8)
+LOWER_STOPS = (0, 1, 2, 3, 8)
 
 
 def remote(src, dst, send_sem, recv_sem, device_id):
@@ -41,11 +46,11 @@
 
 
 def layer_kernel(
-    q_hbm, k_hbm, v_hbm, rates_hbm, decays_ref, fin_hbm, fout_hbm, gain_hbm, w_hbm, o_ref,
+    q_hbm, k_hbm, v_hbm, rates_hbm, decays_ref, fin_hbm, fout_hbm, gain_hbm, w_hbm, o_hbm,
     kv, qh, spare, rates_ref, rate_cols, fin_ref, fout_ref, gain_ref, w_ref,
-    dsend, dpair, tsend, trecv, usend, urecv, ssend, srecv, states, comb, gath,
+    dsend, dpair, tsend, trecv, usend, urecv, ssend, srecv, states, comb, gath, out_ref,
     load_sem, pair_sem, q_send, q_recv, e_send, e_recv, far_send, far_recv, t_send, t_recv,
-    u_send, u_recv, s_send, s_recv, g_send, g_recv,
+    u_send, u_recv, s_send, s_recv, g_send, g_recv, out_sem,
 ):
     place = lax.axis_index("seq")
     head_place = lax.axis_index("head")
@@ -218,7 +223,30 @@
 
     d_copy.start()
 
-    far_copy((1 + z_lo) * pieces - 1).start()
+    def own_piece(c):
+        return lambda: far_copy(c).start()
+
+    def got_piece(i):
+        return lambda: relay_far(i)
+
+    upper_order = [own_piece(2 * pieces - 1 - n) for n in range(pieces)]
+    upper_order += [got_piece(pieces - 1 - n) for n in range(pieces)]
+    lower_order = [own_piece(pieces - 1)]
+    lower_order += [got_piece(pieces - 1 - n) for n in range(pieces)]
+    lower_order += [own_piece(pieces - 2 - n) for n in range(pieces - 1)]
+
+    def send_far(stage):
+        @pl.when(z_lo == 1)
+        def _():
+            for send in upper_order[UPPER_STOPS[stage] : UPPER_STOPS[stage + 1]]:
+                send()
+
+        @pl.when(z_lo == 0)
+        def _():
+            for send in lower_order[LOWER_STOPS[stage] : LOWER_STOPS[stage + 1]]:
+                send()
+
+    send_far(0)
 
     loads[7].wait()
     for i in reversed(range(pieces)):
@@ -246,15 +274,7 @@
     lax.fori_loop(1, COLUMN, start(t_copy), 0)
     trecv[rung] = tsend[rung]
 
-    @pl.when(z_lo == 1)
-    def _():
-        far_copy(2 * pieces - 2).start()
-        far_copy(2 * pieces - 3).start()
-
-    @pl.when(z_lo == 0)
-    def _():
-        relay_far(3)
-
+    send_far(1)
     lax.fori_loop(1, COLUMN, wait_got(t_copy), 0)
 
     def fold_in(r, total):
@@ -267,10 +287,7 @@
 
     lax.fori_loop(1, COLUMNS, start(u_copy), 0)
     urecv[column] = usend[...]
-
-    @pl.when(z_lo == 0)
-    def _():
-        relay_far(2)
+    send_far(2)
 
     slice_rows = pl.ds(pl.multiple_of(rung * (dh // COLUMN), dh // COLUMN), dh // COLUMN)
     state = jnp.concatenate(
@@ -300,19 +317,7 @@
     lax.fori_loop(1, COLUMN, start(s_copy), 0)
     srecv[rung] = ssend[rung]
 
-    @pl.when(z_lo == 1)
-    def _():
-        far_copy(2 * pieces - 4).start()
-        relay_far(3)
-        relay_far(2)
-
-    relay_far(1)
-    relay_far(0)
-
-    @pl.when(z_lo == 0)
-    def _():
-        for i in reversed(range(pieces - 1)):
-            far_copy(i).start()
+    send_far(3)
 
     span = 2 * block_len + ROWS
     first_valid = jnp.where(pair == 0, 2 * block_len, 0)
@@ -400,66 +405,80 @@
     states[0] = srecv[...].reshape(dh, 3 * dh)
     states[1] = (decay_at(2 * pair) * states[0].astype(F32) + dpair[0].astype(F32)).astype(BF16)
 
-    for parity in (1, 0):
-
-        def one(step, _):
-            i = pieces - 1 - step
-            j = i + parity * pieces
-
-            @pl.when(z_lo != parity)
+    def relay(i):
+        got(0, i)
+        if i % 2 == 0:
+            pass_on(2, 0, i, up2).start()
+        pass_on(8, 0, i, twin).start()
+        got(1, i)
+        if i % 2 == 1:
+            pass_on(2, 1, i, down2).start()
+        pass_on(9, 1, i, twin).start()
+        got(3, i)
+        pass_on(5, 3, i, up2).start()
+        pass_on(11, 3, i, twin).start()
+        got(4, i)
+        pass_on(6, 4, i, down2).start()
+        pass_on(12, 4, i, twin).start()
+
+    waited = 2 * pieces
+    for j in (7, 6, 3, 5, 2, 4, 1, 0):
+        parity, i = divmod(j, pieces)
+
+        @pl.when(z_lo != parity)
+        def _():
+            q_copy(i).wait_recv()
+
+        while waited > j:
+            waited -= 1
+            far_copy(waited).wait_recv()
+        finish(j, attend(j), parity)
+        if j in EARLY:
+
+            @pl.when(z_lo == 1)
             def _():
-                q_copy(i).wait_recv()
-
-            far_copy(j).wait_recv()
-            finish(j, attend(j), parity)
-            return 0
-
-        lax.fori_loop(0, pieces, one, 0)
-
-    def relay(step, _):
-        for odd in (1, 0):
-            i = pieces - 2 - 2 * step + odd
-            got(0, i)
-            if odd == 0:
-                pass_on(2, 0, i, up2).start()
-            pass_on(8, 0, i, twin).start()
-            got(1, i)
-            if odd == 1:
-                pass_on(2, 1, i, down2).start()
-            pass_on(9, 1, i, twin).start()
-            got(3, i)
-            pass_on(5, 3, i, up2).start()
-            pass_on(11, 3, i, twin).start()
-            got(4, i)
-            pass_on(6, 4, i, down2).start()
-            pass_on(12, 4, i, twin).start()
-        return 0
-
-    lax.fori_loop(0, pieces // 2, relay, 0)
+                relay(EARLY[j])
+
+    for i in reversed(range(pieces)):
+        if i in EARLY.values():
+
+            @pl.when(z_lo == 0)
+            def _():
+                relay(i)
+
+        else:
+            relay(i)
+
+    loads[10].wait()
+
+    def out_copy(i):
+        return pltpu.make_async_copy(out_ref.at[piece_of(i)], o_hbm.at[piece_of(i)], out_sem.at[i])
+
+    def project(i):
+        for kind in range(7, 15):
+            got(kind, i)
+        row = piece_of(i)
+        total = jnp.zeros((ROWS, out_ref.shape[1]), F32)
+        for g in range(0, HEADS, 2):
+            both = jnp.concatenate([gath[g, row], gath[g + 1, row]], axis=-1)
+            total += dot(both, w_ref[g * dh : (g + 2) * dh, :])
+        out_ref[row, :] = total.astype(BF16)
+        out_copy(i).start()
 
     def last_hop(step, _):
         i = pieces - 1 - step
         for kind in (2, 5, 6):
             got(kind, i)
             pass_on(kind + 8, kind, i, twin).start()
+
+        @pl.when(step > 0)
+        def _():
+            project(i + 1)
+
         return 0
 
     lax.fori_loop(0, pieces, last_hop, 0)
-    loads[10].wait()
-
-    def project(step, _):
-        i = pieces - 1 - step
-        for kind in range(7, 15):
-            got(kind, i)
-        row = piece_of(i)
-        total = jnp.zeros((ROWS, o_ref.shape[1]), F32)
-        for g in range(0, HEADS, 2):
-            both = jnp.concatenate([gath[g, row], gath[g + 1, row]], axis=-1)
-            total += dot(both, w_ref[g * dh : (g + 2) * dh, :])
-        o_ref[row, :] = total.astype(BF16)
-        return 0
-
-    lax.fori_loop(0, pieces, project, 0)
+    project(0)
 
     d_copy.wait_send()
 
@@ -475,6 +494,8 @@
     lax.fori_loop(1, COLUMNS, wait_sent(u_copy), 0)
     lax.fori_loop(1, COLUMN, wait_sent(s_copy), 0)
     lax.fori_loop(0, pieces, drain_gather, 0)
+    for i in range(pieces):
+        out_copy(i).wait()
 
 
 def local(queries, keys, values, rates, decays, fast_in, fast_out, ttt_gain, out_weight):
@@ -490,7 +511,7 @@
         layer_kernel,
         out_shape=jax.ShapeDtypeStruct((block_len, width), BF16),
         in_specs=[hbm, hbm, hbm, hbm, pl.BlockSpec(memory_space=pltpu.SMEM), hbm, hbm, hbm, hbm],
-        out_specs=pl.BlockSpec(memory_space=pltpu.VMEM),
+        out_specs=hbm,
         scratch_shapes=[
             vmem((2, 4 * block_len, dh), BF16),
             vmem((2 * block_len, dh), BF16),
@@ -512,12 +533,13 @@
             vmem((2,) + state_shape, BF16),
             vmem((2, block_len, dh), BF16),
             vmem((HEADS, block_len, dh), BF16),
+            vmem((block_len, width), BF16),
             dma((11,)), dma((2,)),
             dma((pieces,)), dma((pieces,)),
             dma((pieces,)), dma((pieces,)), dma((2 * pieces,)), dma((2 * pieces,)),
             dma((COLUMN,)), dma((COLUMN,)), dma((COLUMNS,)), dma((COLUMNS,)),
             dma((COLUMN,)), dma((COLUMN,)),
-            dma((15, pieces)), dma((15, pieces)),
+            dma((15, pieces)), dma((15, pieces)), dma((pieces,)),
         ],
         compiler_params=pltpu.CompilerParams(
             collective_id=0, has_side_effects=True, vmem_limit_bytes=63 << 20

time: 80.8 us -> 79.4 us (0.983)
  Pallas kernels: 78.7 us -> 77.3 us
    pallas_call x1, Pallas kernels: 78.7 us -> 77.3 us  [local(): pl.pallas_call(layer_kernel, out_shape=jax.ShapeDtypeStruct((block_len, w...]
where the time goes in v3:
time: 79.4 us; the launch traced here: 79.2 us
  Pallas kernels  77.3 us (97%)
  local copies, waits for them, and re-layouts  1.87 us (2%)
    pallas_call x1, Pallas kernels, local(): pl.pallas_call(layer_kernel, out_shape=jax.ShapeDtypeStruct((block_len, w...  77.3 us
    unnamed x1, local copies, waits for them, and re-layouts  1.87 us

profile of v3, /device:TPU:1, one launch (start us, length us, event | category | flops | bytes accessed | tf_op | source)
XLA Modules:
  0.0 79.2 jit_solution(5483735599907594584)
XLA Ops:
  0.0 77.3 %layer.1 = bf16[1024,256]{1,0:T(8,128)(2,1)} custom-call(bf16[1024,256]{1,0:T(8,128)(2,1)} %bitcast.8, bf16[1024,256]{1,0:T(8,128)(2,1)} %bitcast.9, bf16[1024,256]{1,0:T(8,128)(2,1)} %bitcast.10, f32[2,1024]{1,0:T(2,128)} %bitcast.11, f32[2,64]{1,0:T(2,128)} %bitcast.12, bf16[2,128,256]{2,1,0:T(8,128)(2,1)} %fin_hbm.1, bf16[2,128,128]{2,1,0:T(8,128)(2,1)} %fout_hbm.1, ...), custom_call_target="tpu_custom_call" | custom-call | tf_op jit(solution)/shard_map/layer/pallas_call | solution.py:510
  77.4 1.9 %copy.11 = bf16[1,1024,256]{2,1,0:T(8,128)(2,1)} copy(bf16[1,1024,256]{2,1,0:T(8,128)(2,1)} %bitcast.7) | data formatting | bytes 1048576

commit v4 on v3

--- a/solution.py
+++ b/solution.py
@@ -46,11 +46,11 @@
 
 
 def layer_kernel(
-    q_hbm, k_hbm, v_hbm, rates_hbm, decays_ref, fin_hbm, fout_hbm, gain_hbm, w_hbm, o_hbm,
+    q_hbm, k_hbm, v_hbm, rates_hbm, decays_ref, fin_hbm, fout_hbm, gain_hbm, w_hbm, out_ref,
     kv, qh, spare, rates_ref, rate_cols, fin_ref, fout_ref, gain_ref, w_ref,
-    dsend, dpair, tsend, trecv, usend, urecv, ssend, srecv, states, comb, gath, out_ref,
+    dsend, dpair, tsend, trecv, usend, urecv, ssend, srecv, states, comb, gath,
     load_sem, pair_sem, q_send, q_recv, e_send, e_recv, far_send, far_recv, t_send, t_recv,
-    u_send, u_recv, s_send, s_recv, g_send, g_recv, out_sem,
+    u_send, u_recv, s_send, s_recv, g_send, g_recv,
 ):
     place = lax.axis_index("seq")
     head_place = lax.axis_index("head")
@@ -422,7 +422,7 @@
         pass_on(12, 4, i, twin).start()
 
     waited = 2 * pieces
-    for j in (7, 6, 3, 5, 2, 4, 1, 0):
+    for j in (7, 6, 5, 3, 4, 2, 1, 0):
         parity, i = divmod(j, pieces)
 
         @pl.when(z_lo != parity)
@@ -450,9 +450,6 @@
             relay(i)
 
     loads[10].wait()
-
-    def out_copy(i):
-        return pltpu.make_async_copy(out_ref.at[piece_of(i)], o_hbm.at[piece_of(i)], out_sem.at[i])
 
     def project(i):
         for kind in range(7, 15):
@@ -463,7 +460,6 @@
             both = jnp.concatenate([gath[g, row], gath[g + 1, row]], axis=-1)
             total += dot(both, w_ref[g * dh : (g + 2) * dh, :])
         out_ref[row, :] = total.astype(BF16)
-        out_copy(i).start()
 
     def last_hop(step, _):
         i = pieces - 1 - step
@@ -494,8 +490,6 @@
     lax.fori_loop(1, COLUMNS, wait_sent(u_copy), 0)
     lax.fori_loop(1, COLUMN, wait_sent(s_copy), 0)
     lax.fori_loop(0, pieces, drain_gather, 0)
-    for i in range(pieces):
-        out_copy(i).wait()
 
 
 def local(queries, keys, values, rates, decays, fast_in, fast_out, ttt_gain, out_weight):
@@ -509,9 +503,9 @@
     vmem = pltpu.VMEM
     out = pl.pallas_call(
         layer_kernel,
-        out_shape=jax.ShapeDtypeStruct((block_len, width), BF16),
+        out_shape=vmem((block_len, width), BF16),
         in_specs=[hbm, hbm, hbm, hbm, pl.BlockSpec(memory_space=pltpu.SMEM), hbm, hbm, hbm, hbm],
-        out_specs=hbm,
+        out_specs=pl.BlockSpec(memory_space=pltpu.VMEM),
         scratch_shapes=[
             vmem((2, 4 * block_len, dh), BF16),
             vmem((2 * block_len, dh), BF16),
@@ -533,13 +527,12 @@
             vmem((2,) + state_shape, BF16),
             vmem((2, block_len, dh), BF16),
             vmem((HEADS, block_len, dh), BF16),
-            vmem((block_len, width), BF16),
             dma((11,)), dma((2,)),
             dma((pieces,)), dma((pieces,)),
             dma((pieces,)), dma((pieces,)), dma((2 * pieces,)), dma((2 * pieces,)),
             dma((COLUMN,)), dma((COLUMN,)), dma((COLUMNS,)), dma((COLUMNS,)),
             dma((COLUMN,)), dma((COLUMN,)),
-            dma((15, pieces)), dma((15, pieces)), dma((pieces,)),
+            dma((15, pieces)), dma((15, pieces)),
         ],
         compiler_params=pltpu.CompilerParams(
             collective_id=0, has_side_effects=True, vmem_limit_bytes=63 << 20

time: 79.4 us -> 77.5 us (0.976)
  local copies, waits for them, and re-layouts: 1.87 us -> 0.8 us
  Pallas kernels: 77.3 us -> 76.4 us
    unnamed x1, local copies, waits for them, and re-layouts: 1.87 us -> 0.8 us
    pallas_call x1, Pallas kernels: 77.3 us -> 76.4 us  [local(): pl.pallas_call(layer_kernel, out_shape=vmem((block_len, width), BF16), in...]
where the time goes in v4:
time: 77.5 us; the launch traced here: 77.2 us
  Pallas kernels  76.4 us (99%)
  local copies, waits for them, and re-layouts  0.8 us (1%)
    pallas_call x1, Pallas kernels, local(): pl.pallas_call(layer_kernel, out_shape=vmem((block_len, width), BF16), in...  76.4 us

profile of v4, /device:TPU:1, one launch (start us, length us, event | category | flops | bytes accessed | tf_op | source)
XLA Modules:
  0.0 77.2 jit_solution(5778888027273040613)
XLA Ops:
  0.0 76.4 %layer.1 = bf16[1024,256]{1,0:T(8,128)(2,1)S(1)} custom-call(bf16[1024,256]{1,0:T(8,128)(2,1)} %bitcast.8, bf16[1024,256]{1,0:T(8,128)(2,1)} %bitcast.9, bf16[1024,256]{1,0:T(8,128)(2,1)} %bitcast.10, f32[2,1024]{1,0:T(2,128)} %bitcast.11, f32[2,64]{1,0:T(2,128)} %bitcast.12, bf16[2,128,256]{2,1,0:T(8,128)(2,1)} %fin_hbm.1, bf16[2,128,128]{2,1,0:T(8,128)(2,1)} %fout_hbm.1, ...), custom_call_target="tpu_custom_call" | custom-call | tf_op jit(solution)/shard_map/layer/pallas_call | solution.py:504
  76.4 0.8 %copy.11 = bf16[1,1024,256]{2,1,0:T(8,128)(2,1)} copy(bf16[1,1024,256]{2,1,0:T(8,128)(2,1)S(1)} %bitcast.7) | data formatting | bytes 1048576
